TPU v7x, 128 devices: a whole 4x4x4 slice. The times are simulated.
128 devices in a mesh: dp: 16 (over z, x), obj: 8 (over y, core).
Axes of the slice: x: 4, y: 4, z: 4, core: 2. Of those that a mesh axis runs over, the one named last changes fastest.
Arguments:
- object_field: float32 [2, 4096, 4096], P(None, 'dp', 'obj'), may hold values from -6 to 6
- probe_modes: float32 [4, 2, 256, 256], replicated, may hold values from -3 to 3
- amplitude: float32 [768, 256, 256], P(('dp', 'obj')), may hold values from 0.3 to 5
- offsets: int32 [768, 2], P(('dp', 'obj')), may hold values from -128 to 3967, as said below
Outputs:
- object_out: float32 [2, 4096, 4096], P(None, 'dp', 'obj')
- probe_out: float32 [4, 2, 256, 256], replicated
Inputs may be any that keep to these rules, and one draw needn't show every extreme that they name: `offsets`: the position in slot n of a device's 6 slots has its patch centre (offset plus 256 / 2 in both coordinates) inside that device's tile of 256 x 512 object pixels; on every device one position's centre is the tile's first pixel and one is its last pixel.
All inputs are finite; a program needn't handle non-finite values.
Results may differ from a plain program's by a relative error of at most 0.003.
Values may be sent and summed in bfloat16 or wider, within the bound.
A program may use at most 128 MiB of HBM per device.

v0:
```python
import functools

import jax
import jax.numpy as jnp
import ml_dtypes
import numpy as np
from jax import lax
from jax.experimental import pallas as pl
from jax.experimental.pallas import tpu as pltpu
from jax.sharding import Mesh
from jax.sharding import PartitionSpec as P

ITERS = 2
AXES = ("dp_0", "dp_1", "obj_0", "obj_1")
EPSILON = 1e-06
F32, BF16 = jnp.float32, jnp.bfloat16
S = 256
H = S // 2
TR, TC = 256, 512
ER, EC = TR + S, TC + S
MODES, COUNT = 4, 6
ROWS = MODES * 2 * S
HALF, BLOCK, PIECE = ROWS // 2, ROWS // 32, ROWS // 128
MIB = 1 << 20


def dft_tables():
    counter = np.arange(S)
    angle = 2.0 * np.pi * (counter[:, None] * counter[None, :] % S) / S
    re = (np.cos(angle) / 16.0).astype(np.float32).astype(ml_dtypes.bfloat16)
    im = (-np.sin(angle) / 16.0).astype(np.float32).astype(ml_dtypes.bfloat16)
    return np.block([[re, -im], [im, re]]), np.block([[re, im], [-im, re]])


def propagate_body(
    offs, ext, probe, amp, plus, minus, grad, probe_grad, ext32, patch, wave, half, far
):
    n = pl.program_id(0)

    @pl.when(n == 0)
    def _():
        grad[...] = jnp.zeros_like(grad)
        probe_grad[...] = jnp.zeros_like(probe_grad)
        ext32[...] = ext[...].astype(F32)

    row, col = offs[n, 0], offs[n, 1]
    row_base = pl.multiple_of((row // 8) * 8, 8)
    row_shift = row - row_base
    col_block = col // 128
    shift = col - col_block * 128
    rows = pl.ds(row_base, S + 8)

    def cols(i):
        return pl.ds(pl.multiple_of((col_block + i) * 128, 128), 128)

    lane = lax.broadcasted_iota(jnp.int32, (S + 8, 128), 1)
    for p in range(2):
        x = [pltpu.roll(ext32[p, rows, cols(i)], lax.rem(128 - shift, 128), 1) for i in range(3)]
        for i in range(2):
            joined = jnp.where(lane < 128 - shift, x[i], x[i + 1])
            joined = pltpu.roll(joined, lax.rem(S + 8 - row_shift, S + 8), 0)
            patch[p, :, i * 128 : (i + 1) * 128] = joined[:S]
    for m in range(MODES):
        qr, qi = probe[m, 0].astype(F32), probe[m, 1].astype(F32)
        pr, pi = patch[0], patch[1]
        wave[m, :S, :] = (qr * pr - qi * pi).astype(BF16)
        wave[m, S:, :] = (qr * pi + qi * pr).astype(BF16)
        mid = jnp.dot(plus[...], wave[m], preferred_element_type=F32).astype(BF16)
        half[m * S : (m + 1) * S, :S] = mid[:S]
        half[m * S : (m + 1) * S, S:] = mid[S:]
    far[...] = jnp.dot(half[...], minus[...], preferred_element_type=F32)
    intensity = None
    for m in range(MODES):
        fr, fi = far[m * S : (m + 1) * S, :S], far[m * S : (m + 1) * S, S:]
        term = fr * fr + fi * fi
        intensity = term if intensity is None else intensity + term
    ratio = amp[0] / jnp.maximum(jnp.sqrt(intensity), 1.0) - 1.0
    for m in range(MODES):
        wave[m, :S, :] = (far[m * S : (m + 1) * S, :S] * ratio).astype(BF16)
        wave[m, S:, :] = (far[m * S : (m + 1) * S, S:] * ratio).astype(BF16)
        mid = jnp.dot(minus[...], wave[m], preferred_element_type=F32).astype(BF16)
        half[m * S : (m + 1) * S, :S] = mid[:S]
        half[m * S : (m + 1) * S, S:] = mid[S:]
    far[...] = jnp.dot(half[...], plus[...], preferred_element_type=F32)
    gr = gi = None
    for m in range(MODES):
        cr, ci = far[m * S : (m + 1) * S, :S], far[m * S : (m + 1) * S, S:]
        qr, qi = probe[m, 0].astype(F32), probe[m, 1].astype(F32)
        a, b = qr * cr + qi * ci, qr * ci - qi * cr
        gr = a if gr is None else gr + a
        gi = b if gi is None else gi + b
        pr, pi = patch[0], patch[1]
        probe_grad[m, 0] += pr * cr + pi * ci
        probe_grad[m, 1] += pr * ci - pi * cr
    for p, value in enumerate((gr, gi)):
        value = jnp.concatenate([value, jnp.zeros((8, S), F32)], 0)
        x = [
            pltpu.roll(pltpu.roll(value[:, i * 128 : (i + 1) * 128], row_shift, 0), shift, 1)
            for i in range(2)
        ]
        zero = jnp.zeros_like(x[0])
        parts = (
            jnp.where(lane >= shift, x[0], zero),
            jnp.where(lane >= shift, x[1], x[0]),
            jnp.where(lane >= shift, zero, x[1]),
        )
        for i in range(3):
            grad[p, rows, cols(i)] += parts[i]


def propagate(offs, ext, probe_low, amplitude):
    plus, minus = dft_tables()

    def whole(*shape):
        return pl.BlockSpec(shape, lambda n, o: (0,) * len(shape))

    return pl.pallas_call(
        propagate_body,
        grid_spec=pltpu.PrefetchScalarGridSpec(
            num_scalar_prefetch=1,
            grid=(COUNT,),
            in_specs=[
                whole(2, ER, EC),
                whole(MODES, 2, S, S),
                pl.BlockSpec((1, S, S), lambda n, o: (n, 0, 0)),
                whole(2 * S, 2 * S),
                whole(2 * S, 2 * S),
            ],
            out_specs=[whole(2, ER, EC), whole(MODES, 2, S, S)],
            scratch_shapes=[
                pltpu.VMEM((2, ER, EC), F32),
                pltpu.VMEM((2, S, S), F32),
                pltpu.VMEM((MODES, 2 * S, S), BF16),
                pltpu.VMEM((MODES * S, 2 * S), BF16),
                pltpu.VMEM((MODES * S, 2 * S), F32),
            ],
        ),
        out_shape=[
            jax.ShapeDtypeStruct((2, ER, EC), F32),
            jax.ShapeDtypeStruct((MODES, 2, S, S), F32),
        ],
        compiler_params=pltpu.CompilerParams(
            dimension_semantics=("arbitrary",), vmem_limit_bytes=32 * MIB
        ),
        name="propagate",
    )(offs, ext, probe_low, amplitude, jnp.asarray(plus), jnp.asarray(minus))


NEAR = [(a, b) for a in (-1, 0, 1) for b in (-1, 0, 1) if (a, b) != (0, 0)]


class Place:
    def __init__(self):
        self.z, self.x, self.y, self.c = (lax.axis_index(name) for name in AXES)
        self.dp = self.z * 4 + self.x
        self.obj = self.y * 2 + self.c
        self.yz = self.y * 4 + self.z

    def has(self, a, b):
        found = None
        for step, place, count in ((a, self.dp, 16), (b, self.obj, 8)):
            if step:
                test = place > 0 if step < 0 else place < count - 1
                found = test if found is None else jnp.logical_and(found, test)
        return found

    def near(self, a, b):
        dp, obj = self.dp + a, self.obj + b
        return (dp // 4, dp % 4, obj // 2, obj % 2)

    def sibling(self):
        return (self.z, self.x, self.y, 1 - self.c)

    def in_plane(self, d):
        other = (self.yz + d) % 16
        return other, (other % 4, self.x, other // 4, self.c)

    def in_line(self, d):
        other = (self.x + d) % 4
        return other, (self.z, other, self.y, self.c)


def greet(me, everyone):
    barrier = pltpu.get_barrier_semaphore()
    expected = jnp.int32(0)
    for a, b in NEAR:
        there = me.has(a, b)

        @pl.when(there)
        def _():
            pl.semaphore_signal(
                barrier, inc=1, device_id=me.near(a, b), device_id_type=pl.DeviceIdType.MESH
            )

        expected = expected + there.astype(jnp.int32)
    if everyone:
        others = [me.sibling()]
        others += [me.in_plane(d)[1] for d in range(1, 16)]
        others += [me.in_line(d)[1] for d in range(1, 4)]
        for other in others:
            pl.semaphore_signal(
                barrier, inc=1, device_id=other, device_id_type=pl.DeviceIdType.MESH
            )
        expected = expected + len(others)
    pl.semaphore_wait(barrier, expected)


def remote(src, dst, sems, index, device):
    return pltpu.make_async_remote_copy(
        src_ref=src,
        dst_ref=dst,
        send_sem=sems.at[0, index],
        recv_sem=sems.at[1, index],
        device_id=device,
        device_id_type=pl.DeviceIdType.MESH,
    )


def span(step, size, sending):
    if step == 0:
        return pl.ds(H, size)
    if sending:
        return pl.ds(H if step < 0 else size, H)
    return pl.ds(0 if step < 0 else size + H, H)


class Halo:
    def __init__(self, me, ext, sems, plane):
        self.me = me
        self.copies = []
        for i, (a, b) in enumerate(NEAR):
            copy = remote(
                ext.at[plane, span(a, TR, True), span(b, TC, True)],
                ext.at[plane, span(-a, TR, False), span(-b, TC, False)],
                sems,
                plane * 8 + i,
                me.near(a, b),
            )
            self.copies.append((a, b, copy))

    def clear(self, ext, plane):
        for a, b in NEAR:

            @pl.when(jnp.logical_not(self.me.has(a, b)))
            def _():
                part = (plane, span(a, TR, False), span(b, TC, False))
                ext[part] = jnp.zeros(ext.at[part].shape, ext.dtype)

    def start(self):
        for a, b, copy in self.copies:
            pl.when(self.me.has(a, b))(copy.start)

    def wait(self):
        for a, b, copy in self.copies:
            pl.when(self.me.has(-a, -b))(copy.wait_recv)
        for a, b, copy in self.copies:
            pl.when(self.me.has(a, b))(copy.wait_send)


def halo_body(tile, ext, sems):
    me = Place()
    halos = [Halo(me, ext, sems, plane) for plane in range(2)]
    for plane in range(2):
        ext[plane, H : H + TR, H : H + TC] = tile[plane].astype(BF16)
        halos[plane].clear(ext, plane)
    greet(me, False)
    for halo in halos:
        halo.start()
    for halo in halos:
        halo.wait()


def first_halo(tile):
    return pl.pallas_call(
        halo_body,
        out_shape=jax.ShapeDtypeStruct((2, ER, EC), BF16),
        in_specs=[pl.BlockSpec(memory_space=pltpu.VMEM)],
        out_specs=pl.BlockSpec(memory_space=pltpu.VMEM),
        scratch_shapes=[pltpu.SemaphoreType.DMA((2, 16))],
        compiler_params=pltpu.CompilerParams(
            collective_id=0, has_side_effects=True, vmem_limit_bytes=16 * MIB
        ),
        name="first_halo",
    )(tile)


class Fold:
    def __init__(self, me, axis, out, got, sems, plane):
        self.me, self.axis = me, axis
        self.copies = []
        for side, step in enumerate((-1, 1)):
            at = (step, 0) if axis == 0 else (0, step)
            copy = remote(
                out.at[side, plane], got.at[1 - side, plane], sems, plane * 2 + side, me.near(*at)
            )
            self.copies.append((step, at, copy))

    def start(self):
        for step, at, copy in self.copies:
            pl.when(self.me.has(*at))(copy.start)

    def arrive(self, add):
        for side, (step, at, copy) in enumerate(self.copies):
            back = (-at[0], -at[1])

            @pl.when(self.me.has(*back))
            def _():
                copy.wait_recv()
                add(1 - side)

    def finish(self):
        for step, at, copy in self.copies:
            pl.when(self.me.has(*at))(copy.wait_send)


def exchange_body(last, grad, probe_grad, tile, probe, *refs):
    if last:
        tile_out, probe_out = refs[:2]
        refs = refs[2:]
        ext = low_out = halo_sems = None
    else:
        tile_out, probe_out, ext, low_out = refs[:4]
        halo_sems, refs = refs[-1], refs[4:-1]
    (
        col_out, col_got, row_out, row_got, inner,
        pair_out, pair_got, plane_out, plane_got, line_out, line_got, total,
        col_sems, row_sems, pair_sems, plane_sems, line_sems,
        line_back, plane_back, pair_back,
    ) = refs
    me = Place()
    mine, others = me.c * HALF, (1 - me.c) * HALF

    for plane in range(2):
        col_out[0, plane] = grad[plane, :, :H].astype(BF16)
        col_out[1, plane] = grad[plane, :, H + TC :].astype(BF16)
    pair_out[...] = probe_grad[pl.ds(others, HALF), :].astype(BF16)
    greet(me, True)
    folds = [Fold(me, 1, col_out, col_got, col_sems, plane) for plane in range(2)]
    pair = remote(pair_out, pair_got, pair_sems, 0, me.sibling())
    pair.start()
    for fold in folds:
        fold.start()
    power = None
    for m in range(MODES):
        for part in range(2):
            start = (m * 2 + part) * S
            value = probe[start : start + S, :].astype(BF16).astype(F32)
            power = value * value if power is None else power + value * value
    scale = 1.0 / (jnp.max(power, axis=(0, 1), keepdims=True) + EPSILON)
    for plane in range(2):
        inner[plane] = grad[plane, :, H : H + TC]

    pair.wait_recv()
    plane_out[...] = (probe_grad[pl.ds(mine, HALF), :] + pair_got[...].astype(F32)).astype(BF16)
    spread = []
    for d in range(1, 16):
        other, device = me.in_plane(d)
        copy = remote(
            plane_out.at[pl.ds(pl.multiple_of(other * BLOCK, BLOCK), BLOCK)],
            plane_got.at[d - 1],
            plane_sems,
            d - 1,
            device,
        )
        copy.start()
        spread.append(copy)

    row_folds = [Fold(me, 0, row_out, row_got, row_sems, plane) for plane in range(2)]
    for plane in range(2):

        def add_cols(side, plane=plane):
            part = slice(0, H) if side == 0 else slice(TC - H, TC)
            inner[plane, :, part] += col_got[side, plane].astype(F32)

        folds[plane].arrive(add_cols)
        row_out[0, plane] = inner[plane, :H].astype(BF16)
        row_out[1, plane] = inner[plane, H + TR :].astype(BF16)
        row_folds[plane].start()

    for copy in spread:
        copy.wait_recv()
    own = plane_out[pl.ds(pl.multiple_of(me.yz * BLOCK, BLOCK), BLOCK), :].astype(F32)
    for d in range(15):
        own = own + plane_got[d].astype(F32)
    line_out[...] = own.astype(BF16)
    along = []
    for d in range(1, 4):
        other, device = me.in_line(d)
        copy = remote(
            line_out.at[pl.ds(pl.multiple_of(other * PIECE, PIECE), PIECE)],
            line_got.at[d - 1],
            line_sems,
            d - 1,
            device,
        )
        copy.start()
        along.append(copy)

    halos = []
    for plane in range(2):

        def add_rows(side, plane=plane):
            part = slice(H, S) if side == 0 else slice(TR, TR + H)
            inner[plane, part] += row_got[side, plane].astype(F32)

        row_folds[plane].arrive(add_rows)
        value = tile[plane] + inner[plane, H : H + TR] * scale
        tile_out[plane] = value
        if not last:
            ext[plane, H : H + TR, H : H + TC] = value.astype(BF16)
            halo = Halo(me, ext, halo_sems, plane)
            halo.clear(ext, plane)
            halo.start()
            halos.append(halo)

    for copy in along:
        copy.wait_recv()
    own = line_out[pl.ds(pl.multiple_of(me.x * PIECE, PIECE), PIECE), :].astype(F32)
    for d in range(3):
        own = own + line_got[d].astype(F32)
    base = me.c * HALF + me.yz * BLOCK
    piece = pl.ds(pl.multiple_of(base + me.x * PIECE, PIECE), PIECE)
    total[piece, :] = own.astype(BF16)
    backs = []
    for d in range(1, 4):
        copy = remote(total.at[piece], total.at[piece], line_back, d - 1, me.in_line(d)[1])
        copy.start()
        backs.append(copy)
    for copy in backs:
        copy.wait_recv()
    block = pl.ds(pl.multiple_of(base, BLOCK), BLOCK)
    wide = []
    for d in range(1, 16):
        copy = remote(total.at[block], total.at[block], plane_back, d - 1, me.in_plane(d)[1])
        copy.start()
        wide.append(copy)
    for copy in wide:
        copy.wait_recv()
    half = pl.ds(pl.multiple_of(me.c * HALF, HALF), HALF)
    twin = remote(total.at[half], total.at[half], pair_back, 0, me.sibling())
    twin.start()

    def renew(start):
        part = (pl.ds(start, HALF), slice(None))
        value = probe[part] + total[part].astype(F32) / (COUNT * 128)
        probe_out[part] = value
        if not last:
            low_out[part] = value.astype(BF16)

    renew(mine)
    twin.wait_recv()
    renew(others)
    for halo in halos:
        halo.wait()
    for copy in [pair, *spread, *along, *backs, *wide, twin]:
        copy.wait_send()
    for fold in folds + row_folds:
        fold.finish()


def exchange(last, grad, probe_grad, tile, probe):
    sizes = [((2, TR, TC), F32), ((ROWS, S), F32)]
    if not last:
        sizes += [((2, ER, EC), BF16), ((ROWS, S), BF16)]
    vmem = pl.BlockSpec(memory_space=pltpu.VMEM)
    dma = pltpu.SemaphoreType.DMA
    scratch = [
        pltpu.VMEM((2, 2, ER, H), BF16),
        pltpu.VMEM((2, 2, ER, H), BF16),
        pltpu.VMEM((2, 2, H, TC), BF16),
        pltpu.VMEM((2, 2, H, TC), BF16),
        pltpu.VMEM((2, ER, TC), F32),
        pltpu.VMEM((HALF, S), BF16),
        pltpu.VMEM((HALF, S), BF16),
        pltpu.VMEM((HALF, S), BF16),
        pltpu.VMEM((15, BLOCK, S), BF16),
        pltpu.VMEM((BLOCK, S), BF16),
        pltpu.VMEM((3, PIECE, S), BF16),
        pltpu.VMEM((ROWS, S), BF16),
        dma((2, 4)),
        dma((2, 4)),
        dma((2, 1)),
        dma((2, 15)),
        dma((2, 3)),
        dma((2, 3)),
        dma((2, 15)),
        dma((2, 1)),
    ]
    if not last:
        scratch.append(dma((2, 16)))
    return pl.pallas_call(
        functools.partial(exchange_body, last),
        out_shape=[jax.ShapeDtypeStruct(*size) for size in sizes],
        in_specs=[vmem] * 4,
        out_specs=[vmem] * len(sizes),
        scratch_shapes=scratch,
        compiler_params=pltpu.CompilerParams(
            collective_id=2 if last else 1, has_side_effects=True, vmem_limit_bytes=40 * MIB
        ),
        name="last_exchange" if last else "exchange",
    )(grad, probe_grad.reshape(ROWS, S), tile, probe)


def shards(object_field, probe_modes, amplitude, offsets):
    dp = lax.axis_index(AXES[:2])
    obj = lax.axis_index(AXES[2:])
    offs = offsets + H - jnp.stack([dp * TR, obj * TC]).astype(jnp.int32)
    probe = probe_modes.reshape(ROWS, S)
    tile = object_field
    ext = first_halo(tile)
    low = probe.astype(BF16)
    for turn in range(ITERS):
        grad, probe_grad = propagate(offs, ext, low.reshape(MODES, 2, S, S), amplitude)
        last = turn + 1 == ITERS
        results = exchange(last, grad, probe_grad, tile, probe)
        if last:
            tile, probe = results
        else:
            tile, probe, ext, low = results
    return tile, probe.reshape(MODES, 2, S, S)


def solution(mesh):
    split = Mesh(mesh.devices.reshape(4, 4, 4, 2), AXES)
    return jax.shard_map(
        shards,
        mesh=split,
        in_specs=(
            P(None, AXES[:2], AXES[2:]),
            P(),
            P(AXES, None, None),
            P(AXES, None),
        ),
        out_specs=(P(None, AXES[:2], AXES[2:]), P()),
        check_vma=False,
    )
```

profile of v0, /device:TPU:1, one launch (start us, length us, event | category | flops | bytes accessed | tf_op | source)
XLA Modules:
  0.0 151.6 jit_solution(7391409247982915273)
XLA Ops:
  0.6 0.0 copy-start.2
  0.6 0.1 pad_add_fusion
  0.7 0.8 copy.10
  1.6 0.0 copy-start.1
  1.6 0.0 copy-start.3
  1.6 0.0 copy-start.4
  1.6 1.9 %convert_element_type.4.probe = bf16[4,2,256,256]{3,2,1,0:T(8,128)(2,1)S(1)} convert(f32[4,2,256,256]{3,2,1,0:T(8,128)} %param.9) | non-fusion elementwise | flops 524288 | bytes 3145728 | tf_op jit(solution)/shard_map/convert_element_type | solution.py:511
  3.4 0.0 copy-done.2
  3.5 13.2 %first_halo.1.ext = bf16[2,512,768]{2,1,0:T(8,128)(2,1)S(1)} custom-call(f32[2,256,512]{2,1,0:T(8,128)S(1)} %copy-done.2), custom_call_target="tpu_custom_call" | custom-call | tf_op jit(solution)/shard_map/first_halo/pallas_call | solution.py:274
  16.7 0.0 copy-done.1
  16.7 0.0 copy-done.3
  16.7 0.0 copy-done.4
  16.7 0.0 copy-start
  16.7 24.2 %propagate.2 = (f32[2,512,768]{2,1,0:T(8,128)S(1)}, f32[4,2,256,256]{3,2,1,0:T(8,128)S(1)}) custom-call(s32[6,2]{1,0:T(8,128)S(1)} %add_subtract_fusion.offs, bf16[2,512,768]{2,1,0:T(8,128)(2,1)S(1)} %first_halo.1.ext, bf16[4,2,256,256]{3,2,1,0:T(8,128)(2,1)S(1)} %convert_element_type.4.probe, f32[6,256,256]{2,1,0:T(8,128)S(1)} %copy-done.1, ...), custom_call_target="tpu_custom_call" | custom-call | tf_op jit(solution)/shard_map/propagate/pallas_call | solution.py:117
  41.0 0.0 copy-done
  41.0 46.6 %exchange.1 = (f32[2,256,512]{2,1,0:T(8,128)S(1)}, f32[2048,256]{1,0:T(8,128)S(1)}, bf16[2,512,768]{2,1,0:T(8,128)(2,1)S(1)}, bf16[2048,256]{1,0:T(8,128)(2,1)S(1)}) custom-call(f32[2,512,768]{2,1,0:T(8,128)S(1)} %get-tuple-element.12.grad, f32[2048,256]{1,0:T(8,128)S(1)} %bitcast.10, f32[2,256,512]{2,1,0:T(8,128)S(1)} %copy-done.2, f32[2048,256]{1,0:T(8,128)S(1)} %bitcast.7), custom_call_target="tpu_custom_call" | custom-call | tf_op jit(solution)/shard_map/exchange/pallas_call | solution.py:491
  87.6 23.7 %propagate.3 = (f32[2,512,768]{2,1,0:T(8,128)S(1)}, f32[4,2,256,256]{3,2,1,0:T(8,128)S(1)}) custom-call(s32[6,2]{1,0:T(8,128)S(1)} %add_subtract_fusion.offs, bf16[2,512,768]{2,1,0:T(8,128)(2,1)S(1)} %get-tuple-element.14.ext, bf16[4,2,256,256]{3,2,1,0:T(8,128)(2,1)S(1)} %bitcast.11, f32[6,256,256]{2,1,0:T(8,128)S(1)} %copy-done.1, ...), custom_call_target="tpu_custom_call" | custom-call | tf_op jit(solution)/shard_map/propagate/pallas_call | solution.py:117
  111.3 38.0 %last_exchange.1 = (f32[2,256,512]{2,1,0:T(8,128)S(1)}, f32[2048,256]{1,0:T(8,128)S(1)}) custom-call(f32[2,512,768]{2,1,0:T(8,128)S(1)} %get-tuple-element.16.grad, f32[2048,256]{1,0:T(8,128)S(1)} %bitcast.9, f32[2,256,512]{2,1,0:T(8,128)S(1)} %get-tuple-element.18.tile, f32[2048,256]{1,0:T(8,128)S(1)} %get-tuple-element.19.probe), custom_call_target="tpu_custom_call" | custom-call | tf_op jit(solution)/shard_map/last_exchange/pallas_call | solution.py:491
  149.3 1.0 copy.13
  150.3 1.3 copy.14
  (1 shorter events, 0.0 us)
Async XLA Ops:
  0.6 2.8 %copy-start.2 = (f32[2,256,512]{2,1,0:T(8,128)S(1)}, f32[2,256,512]{2,1,0:T(8,128)}, u32[]{:S(2)}) copy-start(f32[2,256,512]{2,1,0:T(8,128)} %tile.3) | copy-start | bytes 3145732
  1.6 15.1 %copy-start.1 = (f32[6,256,256]{2,1,0:T(8,128)S(1)}, f32[6,256,256]{2,1,0:T(8,128)}, u32[]{:S(2)}) copy-start(f32[6,256,256]{2,1,0:T(8,128)} %amp.3) | copy-start | bytes 4718596
  1.6 15.1 %copy-start.3 = (bf16[512,512]{1,0:T(8,128)(2,1)S(1)}, bf16[512,512]{1,0:T(8,128)(2,1)}, u32[]{:S(2)}) copy-start(bf16[512,512]{1,0:T(8,128)(2,1)} %constant.30.clone.minus) | copy-start | bytes 1572868
  1.6 15.1 %copy-start.4 = (bf16[512,512]{1,0:T(8,128)(2,1)S(1)}, bf16[512,512]{1,0:T(8,128)(2,1)}, u32[]{:S(2)}) copy-start(bf16[512,512]{1,0:T(8,128)(2,1)} %constant.29.clone.plus) | copy-start | bytes 1572868
  16.7 24.3 %copy-start = (f32[4,2,256,256]{3,2,1,0:T(8,128)S(1)}, f32[4,2,256,256]{3,2,1,0:T(8,128)}, u32[]{:S(2)}) copy-start(f32[4,2,256,256]{3,2,1,0:T(8,128)} %param.9) | copy-start | bytes 6291460
where the time goes:
time: 152 us
  Pallas kernels  146 us (96%)
  local copies, waits for them, and re-layouts  3.15 us (2%)
  other arithmetic  1.94 us (1%)
    pallas_call x2, Pallas kernels, exchange(): pl.pallas_call(functools.partial(exchange_body, last), out_shape=[jax.Sha...  84.6 us
    pallas_call x2, Pallas kernels, propagate(): pl.pallas_call(propagate_body, grid_spec=pltpu.PrefetchScalarGridSpec(num...  47.9 us
    pallas_call x1, Pallas kernels, first_halo(): pl.pallas_call(halo_body, out_shape=jax.ShapeDtypeStruct((2, ER, EC), BF1...  13.2 us
    unnamed x13, local copies, waits for them, and re-layouts  3.15 us

commit v1 on v0

--- a/solution.py
+++ b/solution.py
@@ -20,7 +20,23 @@
 ER, EC = TR + S, TC + S
 MODES, COUNT = 4, 6
 ROWS = MODES * 2 * S
-HALF, BLOCK, PIECE = ROWS // 2, ROWS // 32, ROWS // 128
+CHUNKS = 2
+CHUNK = ROWS // CHUNKS
+HALF, BLOCK = CHUNK // 2, CHUNK // 32
+ORDER = (
+    "line0",
+    "line1",
+    "back0",
+    "back1",
+    "rows0",
+    "rows1",
+    "twin0",
+    "own0",
+    "twin1",
+    "own1",
+    "rest0",
+    "rest1",
+)
 MIB = 1 << 20
 
 
@@ -33,15 +49,26 @@
 
 
 def propagate_body(
-    offs, ext, probe, amp, plus, minus, grad, probe_grad, ext32, patch, wave, half, far
+    offs, ext, probe_in, amp, plus, minus, grad, probe_grad, ext32, probe, patch, wave, half, far
 ):
     n = pl.program_id(0)
 
+    def by_rows(ref, value):
+        @pl.loop(0, ref.shape[0] // 64)
+        def _(i):
+            rows = pl.ds(i * 64, 64)
+            ref[rows] = value(rows)
+
     @pl.when(n == 0)
     def _():
-        grad[...] = jnp.zeros_like(grad)
-        probe_grad[...] = jnp.zeros_like(probe_grad)
-        ext32[...] = ext[...].astype(F32)
+        for p in range(2):
+            by_rows(grad.at[p], lambda rows: jnp.zeros((64, EC), F32))
+            by_rows(ext32.at[p], lambda rows: ext[p, rows].astype(F32))
+            for m in range(MODES):
+                by_rows(probe_grad.at[m, p], lambda rows: jnp.zeros((64, S), F32))
+                by_rows(
+                    probe.at[m, p], lambda rows: probe_in[m, p, rows].astype(BF16).astype(F32)
+                )
 
     row, col = offs[n, 0], offs[n, 1]
     row_base = pl.multiple_of((row // 8) * 8, 8)
@@ -61,7 +88,7 @@
             joined = pltpu.roll(joined, lax.rem(S + 8 - row_shift, S + 8), 0)
             patch[p, :, i * 128 : (i + 1) * 128] = joined[:S]
     for m in range(MODES):
-        qr, qi = probe[m, 0].astype(F32), probe[m, 1].astype(F32)
+        qr, qi = probe[m, 0], probe[m, 1]
         pr, pi = patch[0], patch[1]
         wave[m, :S, :] = (qr * pr - qi * pi).astype(BF16)
         wave[m, S:, :] = (qr * pi + qi * pr).astype(BF16)
@@ -74,7 +101,7 @@
         fr, fi = far[m * S : (m + 1) * S, :S], far[m * S : (m + 1) * S, S:]
         term = fr * fr + fi * fi
         intensity = term if intensity is None else intensity + term
-    ratio = amp[0] / jnp.maximum(jnp.sqrt(intensity), 1.0) - 1.0
+    ratio = amp[0] * jnp.minimum(lax.rsqrt(intensity), 1.0) - 1.0
     for m in range(MODES):
         wave[m, :S, :] = (far[m * S : (m + 1) * S, :S] * ratio).astype(BF16)
         wave[m, S:, :] = (far[m * S : (m + 1) * S, S:] * ratio).astype(BF16)
@@ -85,7 +112,7 @@
     gr = gi = None
     for m in range(MODES):
         cr, ci = far[m * S : (m + 1) * S, :S], far[m * S : (m + 1) * S, S:]
-        qr, qi = probe[m, 0].astype(F32), probe[m, 1].astype(F32)
+        qr, qi = probe[m, 0], probe[m, 1]
         a, b = qr * cr + qi * ci, qr * ci - qi * cr
         gr = a if gr is None else gr + a
         gi = b if gi is None else gi + b
@@ -108,7 +135,7 @@
             grad[p, rows, cols(i)] += parts[i]
 
 
-def propagate(offs, ext, probe_low, amplitude):
+def propagate(offs, ext, probe, amplitude):
     plus, minus = dft_tables()
 
     def whole(*shape):
@@ -129,6 +156,7 @@
             out_specs=[whole(2, ER, EC), whole(MODES, 2, S, S)],
             scratch_shapes=[
                 pltpu.VMEM((2, ER, EC), F32),
+                pltpu.VMEM((MODES, 2, S, S), F32),
                 pltpu.VMEM((2, S, S), F32),
                 pltpu.VMEM((MODES, 2 * S, S), BF16),
                 pltpu.VMEM((MODES * S, 2 * S), BF16),
@@ -143,7 +171,7 @@
             dimension_semantics=("arbitrary",), vmem_limit_bytes=32 * MIB
         ),
         name="propagate",
-    )(offs, ext, probe_low, amplitude, jnp.asarray(plus), jnp.asarray(minus))
+    )(offs, ext, probe, amplitude, jnp.asarray(plus), jnp.asarray(minus))
 
 
 NEAR = [(a, b) for a in (-1, 0, 1) for b in (-1, 0, 1) if (a, b) != (0, 0)]
@@ -180,7 +208,7 @@
         return other, (self.z, other, self.y, self.c)
 
 
-def greet(me, everyone):
+def signal_all(me, everyone):
     barrier = pltpu.get_barrier_semaphore()
     expected = jnp.int32(0)
     for a, b in NEAR:
@@ -202,7 +230,11 @@
                 barrier, inc=1, device_id=other, device_id_type=pl.DeviceIdType.MESH
             )
         expected = expected + len(others)
-    pl.semaphore_wait(barrier, expected)
+    return expected
+
+
+def wait_all(expected):
+    pl.semaphore_wait(pltpu.get_barrier_semaphore(), expected)
 
 
 def remote(src, dst, sems, index, device):
@@ -259,11 +291,12 @@
 
 def halo_body(tile, ext, sems):
     me = Place()
+    expected = signal_all(me, False)
     halos = [Halo(me, ext, sems, plane) for plane in range(2)]
     for plane in range(2):
         ext[plane, H : H + TR, H : H + TC] = tile[plane].astype(BF16)
         halos[plane].clear(ext, plane)
-    greet(me, False)
+    wait_all(expected)
     for halo in halos:
         halo.start()
     for halo in halos:
@@ -313,33 +346,148 @@
             pl.when(self.me.has(*at))(copy.wait_send)
 
 
+class Probe:
+    def __init__(self, me, chunk, probe_grad, total, bufs, sems):
+        self.me, self.chunk, self.source, self.total = me, chunk, probe_grad, total
+        self.pair_out, self.pair_got, self.plane_out, self.plane_got, self.line_got = (
+            buf.at[chunk] for buf in bufs
+        )
+        self.pair_sems, self.plane_sems, self.line_sems, self.back_sems, self.twin_sems = sems
+        start = chunk * CHUNK
+        self.mine = pl.multiple_of(start + me.c * HALF, HALF)
+        self.others = pl.multiple_of(start + (1 - me.c) * HALF, HALF)
+        self.sent = []
+
+    def go(self, copies):
+        for copy in copies:
+            copy.start()
+        self.sent += copies
+        return copies
+
+    def cast(self):
+        self.pair_out[...] = self.source[pl.ds(self.others, HALF), :].astype(BF16)
+
+    def pair(self):
+        self.pairs = self.go(
+            [remote(self.pair_out, self.pair_got, self.pair_sems, self.chunk, self.me.sibling())]
+        )
+
+    def plane(self):
+        self.pairs[0].wait_recv()
+        own = self.source[pl.ds(self.mine, HALF), :]
+        self.plane_out[...] = (own + self.pair_got[...].astype(F32)).astype(BF16)
+        copies = []
+        for d in range(1, 16):
+            other, device = self.me.in_plane(d)
+            copies.append(
+                remote(
+                    self.plane_out.at[pl.ds(pl.multiple_of(other * BLOCK, BLOCK), BLOCK)],
+                    self.plane_got.at[d - 1],
+                    self.plane_sems,
+                    self.chunk * 15 + d - 1,
+                    device,
+                )
+            )
+        self.planes = self.go(copies)
+
+    def line(self):
+        for copy in self.planes:
+            copy.wait_recv()
+        own = self.plane_out[pl.ds(pl.multiple_of(self.me.yz * BLOCK, BLOCK), BLOCK), :].astype(F32)
+        for d in range(15):
+            own = own + self.plane_got[d].astype(F32)
+        slot = self.line_got.at[self.me.x]
+        slot[...] = own.astype(BF16)
+        self.lines = self.go(
+            [
+                remote(slot, slot, self.line_sems, self.chunk * 3 + d - 1, self.me.in_line(d)[1])
+                for d in range(1, 4)
+            ]
+        )
+
+    def back(self):
+        for copy in self.lines:
+            copy.wait_recv()
+        value = self.line_got[0].astype(F32)
+        for d in range(1, 4):
+            value = value + self.line_got[d].astype(F32)
+        start = pl.multiple_of(self.mine + self.me.yz * BLOCK, BLOCK)
+        block = self.total.at[pl.ds(start, BLOCK)]
+        block[...] = value.astype(BF16)
+        self.backs = self.go(
+            [
+                remote(block, block, self.back_sems, self.chunk * 15 + d - 1, self.me.in_plane(d)[1])
+                for d in range(1, 16)
+            ]
+        )
+
+    def twin(self):
+        for copy in self.backs:
+            copy.wait_recv()
+        half = self.total.at[pl.ds(self.mine, HALF)]
+        self.twins = self.go([remote(half, half, self.twin_sems, self.chunk, self.me.sibling())])
+
+    def renew(self, own, probe, probe_out):
+        if not own:
+            self.twins[0].wait_recv()
+        if probe_out is None:
+            return
+        part = (pl.ds(self.mine if own else self.others, HALF), slice(None))
+        value = probe[part] + self.total[part].astype(F32) / (COUNT * 128)
+        probe_out[part] = value
+
+    def finish(self):
+        for copy in self.sent:
+            copy.wait_send()
+
+
 def exchange_body(last, grad, probe_grad, tile, probe, *refs):
     if last:
-        tile_out, probe_out = refs[:2]
+        tile_out, total = refs[:2]
         refs = refs[2:]
-        ext = low_out = halo_sems = None
+        ext = probe_out = halo_sems = None
     else:
-        tile_out, probe_out, ext, low_out = refs[:4]
-        halo_sems, refs = refs[-1], refs[4:-1]
-    (
-        col_out, col_got, row_out, row_got, inner,
-        pair_out, pair_got, plane_out, plane_got, line_out, line_got, total,
-        col_sems, row_sems, pair_sems, plane_sems, line_sems,
-        line_back, plane_back, pair_back,
-    ) = refs
+        tile_out, probe_out, ext = refs[:3]
+        halo_sems, total, refs = refs[-2], refs[-1], refs[3:-2]
+    col_out, col_got, row_out, row_got, inner = refs[:5]
+    col_sems, row_sems = refs[10:12]
     me = Place()
-    mine, others = me.c * HALF, (1 - me.c) * HALF
-
+    expected = signal_all(me, True)
+    chunks = [Probe(me, i, probe_grad, total, refs[5:10], refs[12:]) for i in range(CHUNKS)]
+    for chunk in chunks:
+        chunk.cast()
     for plane in range(2):
         col_out[0, plane] = grad[plane, :, :H].astype(BF16)
         col_out[1, plane] = grad[plane, :, H + TC :].astype(BF16)
-    pair_out[...] = probe_grad[pl.ds(others, HALF), :].astype(BF16)
-    greet(me, True)
+    wait_all(expected)
     folds = [Fold(me, 1, col_out, col_got, col_sems, plane) for plane in range(2)]
-    pair = remote(pair_out, pair_got, pair_sems, 0, me.sibling())
-    pair.start()
+    row_folds = [Fold(me, 0, row_out, row_got, row_sems, plane) for plane in range(2)]
+    halos = []
+    for chunk in chunks:
+        chunk.pair()
     for fold in folds:
         fold.start()
+    if not last:
+        for plane in range(2):
+            halos.append(Halo(me, ext, halo_sems, plane))
+            halos[-1].clear(ext, plane)
+    for plane in range(2):
+        inner[plane] = grad[plane, :, H : H + TC]
+    for chunk in chunks:
+        chunk.plane()
+
+    def fold_cols(plane):
+        def add(side):
+            part = slice(0, H) if side == 0 else slice(TC - H, TC)
+            inner[plane, :, part] += col_got[side, plane].astype(F32)
+
+        folds[plane].arrive(add)
+        row_out[0, plane] = inner[plane, :H].astype(BF16)
+        row_out[1, plane] = inner[plane, H + TR :].astype(BF16)
+        row_folds[plane].start()
+
+    for plane in range(2):
+        fold_cols(plane)
     power = None
     for m in range(MODES):
         for part in range(2):
@@ -347,121 +495,45 @@
             value = probe[start : start + S, :].astype(BF16).astype(F32)
             power = value * value if power is None else power + value * value
     scale = 1.0 / (jnp.max(power, axis=(0, 1), keepdims=True) + EPSILON)
-    for plane in range(2):
-        inner[plane] = grad[plane, :, H : H + TC]
-
-    pair.wait_recv()
-    plane_out[...] = (probe_grad[pl.ds(mine, HALF), :] + pair_got[...].astype(F32)).astype(BF16)
-    spread = []
-    for d in range(1, 16):
-        other, device = me.in_plane(d)
-        copy = remote(
-            plane_out.at[pl.ds(pl.multiple_of(other * BLOCK, BLOCK), BLOCK)],
-            plane_got.at[d - 1],
-            plane_sems,
-            d - 1,
-            device,
-        )
-        copy.start()
-        spread.append(copy)
-
-    row_folds = [Fold(me, 0, row_out, row_got, row_sems, plane) for plane in range(2)]
-    for plane in range(2):
-
-        def add_cols(side, plane=plane):
-            part = slice(0, H) if side == 0 else slice(TC - H, TC)
-            inner[plane, :, part] += col_got[side, plane].astype(F32)
-
-        folds[plane].arrive(add_cols)
-        row_out[0, plane] = inner[plane, :H].astype(BF16)
-        row_out[1, plane] = inner[plane, H + TR :].astype(BF16)
-        row_folds[plane].start()
-
-    for copy in spread:
-        copy.wait_recv()
-    own = plane_out[pl.ds(pl.multiple_of(me.yz * BLOCK, BLOCK), BLOCK), :].astype(F32)
-    for d in range(15):
-        own = own + plane_got[d].astype(F32)
-    line_out[...] = own.astype(BF16)
-    along = []
-    for d in range(1, 4):
-        other, device = me.in_line(d)
-        copy = remote(
-            line_out.at[pl.ds(pl.multiple_of(other * PIECE, PIECE), PIECE)],
-            line_got.at[d - 1],
-            line_sems,
-            d - 1,
-            device,
-        )
-        copy.start()
-        along.append(copy)
-
-    halos = []
-    for plane in range(2):
-
-        def add_rows(side, plane=plane):
+
+    def fold_rows(plane):
+        def add(side):
             part = slice(H, S) if side == 0 else slice(TR, TR + H)
             inner[plane, part] += row_got[side, plane].astype(F32)
 
-        row_folds[plane].arrive(add_rows)
-        value = tile[plane] + inner[plane, H : H + TR] * scale
-        tile_out[plane] = value
-        if not last:
+        row_folds[plane].arrive(add)
+        value = inner[plane, H : H + TR] * scale
+        if last:
+            tile_out[plane] = value
+        else:
+            value = tile[plane] + value
+            tile_out[plane] = value
             ext[plane, H : H + TR, H : H + TC] = value.astype(BF16)
-            halo = Halo(me, ext, halo_sems, plane)
-            halo.clear(ext, plane)
-            halo.start()
-            halos.append(halo)
-
-    for copy in along:
-        copy.wait_recv()
-    own = line_out[pl.ds(pl.multiple_of(me.x * PIECE, PIECE), PIECE), :].astype(F32)
-    for d in range(3):
-        own = own + line_got[d].astype(F32)
-    base = me.c * HALF + me.yz * BLOCK
-    piece = pl.ds(pl.multiple_of(base + me.x * PIECE, PIECE), PIECE)
-    total[piece, :] = own.astype(BF16)
-    backs = []
-    for d in range(1, 4):
-        copy = remote(total.at[piece], total.at[piece], line_back, d - 1, me.in_line(d)[1])
-        copy.start()
-        backs.append(copy)
-    for copy in backs:
-        copy.wait_recv()
-    block = pl.ds(pl.multiple_of(base, BLOCK), BLOCK)
-    wide = []
-    for d in range(1, 16):
-        copy = remote(total.at[block], total.at[block], plane_back, d - 1, me.in_plane(d)[1])
-        copy.start()
-        wide.append(copy)
-    for copy in wide:
-        copy.wait_recv()
-    half = pl.ds(pl.multiple_of(me.c * HALF, HALF), HALF)
-    twin = remote(total.at[half], total.at[half], pair_back, 0, me.sibling())
-    twin.start()
-
-    def renew(start):
-        part = (pl.ds(start, HALF), slice(None))
-        value = probe[part] + total[part].astype(F32) / (COUNT * 128)
-        probe_out[part] = value
-        if not last:
-            low_out[part] = value.astype(BF16)
-
-    renew(mine)
-    twin.wait_recv()
-    renew(others)
+            halos[plane].start()
+
+    for step in ORDER:
+        kind, index = step[:-1], int(step[-1])
+        if kind == "rows":
+            fold_rows(index)
+        elif kind in ("line", "back", "twin"):
+            if index < CHUNKS:
+                getattr(chunks[index], kind)()
+        elif kind == "own" and index < CHUNKS:
+            chunks[index].renew(True, probe, probe_out)
+        elif kind == "rest" and index < CHUNKS:
+            chunks[index].renew(False, probe, probe_out)
     for halo in halos:
         halo.wait()
-    for copy in [pair, *spread, *along, *backs, *wide, twin]:
-        copy.wait_send()
+    for chunk in chunks:
+        chunk.finish()
     for fold in folds + row_folds:
         fold.finish()
 
 
 def exchange(last, grad, probe_grad, tile, probe):
-    sizes = [((2, TR, TC), F32), ((ROWS, S), F32)]
+    sizes = [((2, TR, TC), F32), ((ROWS, S), BF16 if last else F32)]
     if not last:
-        sizes += [((2, ER, EC), BF16), ((ROWS, S), BF16)]
+        sizes += [((2, ER, EC), BF16)]
     vmem = pl.BlockSpec(memory_space=pltpu.VMEM)
     dma = pltpu.SemaphoreType.DMA
     scratch = [
@@ -470,24 +542,21 @@
         pltpu.VMEM((2, 2, H, TC), BF16),
         pltpu.VMEM((2, 2, H, TC), BF16),
         pltpu.VMEM((2, ER, TC), F32),
-        pltpu.VMEM((HALF, S), BF16),
-        pltpu.VMEM((HALF, S), BF16),
-        pltpu.VMEM((HALF, S), BF16),
-        pltpu.VMEM((15, BLOCK, S), BF16),
-        pltpu.VMEM((BLOCK, S), BF16),
-        pltpu.VMEM((3, PIECE, S), BF16),
-        pltpu.VMEM((ROWS, S), BF16),
+        pltpu.VMEM((CHUNKS, HALF, S), BF16),
+        pltpu.VMEM((CHUNKS, HALF, S), BF16),
+        pltpu.VMEM((CHUNKS, HALF, S), BF16),
+        pltpu.VMEM((CHUNKS, 15, BLOCK, S), BF16),
+        pltpu.VMEM((CHUNKS, 4, BLOCK, S), BF16),
         dma((2, 4)),
         dma((2, 4)),
-        dma((2, 1)),
-        dma((2, 15)),
-        dma((2, 3)),
-        dma((2, 3)),
-        dma((2, 15)),
-        dma((2, 1)),
+        dma((2, CHUNKS)),
+        dma((2, 15 * CHUNKS)),
+        dma((2, 3 * CHUNKS)),
+        dma((2, 15 * CHUNKS)),
+        dma((2, CHUNKS)),
     ]
     if not last:
-        scratch.append(dma((2, 16)))
+        scratch += [dma((2, 16)), pltpu.VMEM((ROWS, S), BF16)]
     return pl.pallas_call(
         functools.partial(exchange_body, last),
         out_shape=[jax.ShapeDtypeStruct(*size) for size in sizes],
@@ -508,15 +577,15 @@
     probe = probe_modes.reshape(ROWS, S)
     tile = object_field
     ext = first_halo(tile)
-    low = probe.astype(BF16)
     for turn in range(ITERS):
-        grad, probe_grad = propagate(offs, ext, low.reshape(MODES, 2, S, S), amplitude)
+        grad, probe_grad = propagate(offs, ext, probe.reshape(MODES, 2, S, S), amplitude)
         last = turn + 1 == ITERS
         results = exchange(last, grad, probe_grad, tile, probe)
         if last:
-            tile, probe = results
+            tile = tile + results[0]
+            probe = probe + results[1].astype(F32) / (COUNT * 128)
         else:
-            tile, probe, ext, low = results
+            tile, probe, ext = results
     return tile, probe.reshape(MODES, 2, S, S)
 
 

time: 152 us -> 143 us (0.941)
  Pallas kernels: 146 us -> 135 us
    pallas_call x2, Pallas kernels: 84.6 us -> 75.1 us  [exchange(): pl.pallas_call(functools.partial(exchange_body, last), out_shape=[jax.Sha...]
    add x0 -> x2, other arithmetic: none -> 2.74 us  [the longest x1 1.56 us: shards(): probe = probe + results[1].astype(F32) / (COUNT * 128)]
    convert_element_type x1 -> x0, other arithmetic: 1.86 us -> none  [shards(): low = probe.astype(BF16)]
    unnamed x13 -> x17, local copies, waits for them, and re-layouts: 3.15 us -> 4.59 us
where the time goes in v1:
time: 143 us
  Pallas kernels  135 us (94%)
  local copies, waits for them, and re-layouts  4.59 us (3%)
  other arithmetic  2.82 us (2%)
    pallas_call x2, Pallas kernels, exchange(): pl.pallas_call(functools.partial(exchange_body, last), out_shape=[jax.Sha...  75.1 us
    pallas_call x2, Pallas kernels, propagate(): pl.pallas_call(propagate_body, grid_spec=pltpu.PrefetchScalarGridSpec(num...  46.9 us
    pallas_call x1, Pallas kernels, first_halo(): pl.pallas_call(halo_body, out_shape=jax.ShapeDtypeStruct((2, ER, EC), BF1...  13 us
    unnamed x17, local copies, waits for them, and re-layouts  4.59 us

profile of v1, /device:TPU:1, one launch (start us, length us, event | category | flops | bytes accessed | tf_op | source)
XLA Modules:
  0.0 143.2 jit_solution(10351823961088875597)
XLA Ops:
  0.6 0.0 copy-start
  0.6 0.1 pad_add_fusion
  0.7 0.9 copy.10
  1.6 0.0 copy-start.3
  1.6 1.2 copy-done.3
  2.9 0.0 copy-start.5
  2.9 13.0 %first_halo.1.ext = bf16[2,512,768]{2,1,0:T(8,128)(2,1)S(1)} custom-call(f32[2,256,512]{2,1,0:T(8,128)S(1)} %copy-done.3), custom_call_target="tpu_custom_call" | custom-call | tf_op jit(solution)/shard_map/first_halo/pallas_call | solution.py:307
  15.9 0.0 copy-done
  15.9 0.0 copy-done.5
  15.9 0.0 copy-start.1
  15.9 1.4 copy-done.1
  17.3 0.0 copy-start.6
  17.3 1.0 copy-done.6
  18.3 0.0 copy-start.4
  18.3 23.6 %propagate.2 = (f32[2,512,768]{2,1,0:T(8,128)S(1)}, f32[4,2,256,256]{3,2,1,0:T(8,128)S(1)}) custom-call(s32[6,2]{1,0:T(8,128)S(1)} %add_subtract_fusion.offs, bf16[2,512,768]{2,1,0:T(8,128)(2,1)S(1)} %first_halo.1.ext, f32[4,2,256,256]{3,2,1,0:T(8,128)S(1)} %copy-done, f32[6,256,256]{2,1,0:T(8,128)S(1)} %copy-done.1, bf16[512,512]{1,0:T(8,128)(2,1)S(1)} %copy-done.6, ...), custom_call_target="tpu_custom_call" | custom-call | tf_op jit(solution)/shard_map/propagate/pallas_call | solution.py:144
  42.0 0.0 copy-done.4
  42.0 0.0 copy-start.2
  42.0 0.0 copy-start.7
  42.0 45.0 %exchange.1 = (f32[2,256,512]{2,1,0:T(8,128)S(1)}, f32[2048,256]{1,0:T(8,128)S(1)}, bf16[2,512,768]{2,1,0:T(8,128)(2,1)S(1)}) custom-call(f32[2,512,768]{2,1,0:T(8,128)S(1)} %get-tuple-element.11.grad, f32[2048,256]{1,0:T(8,128)S(1)} %bitcast.10, f32[2,256,512]{2,1,0:T(8,128)S(1)} %copy-done.4, f32[2048,256]{1,0:T(8,128)S(1)} %bitcast.8), custom_call_target="tpu_custom_call" | custom-call | tf_op jit(solution)/shard_map/exchange/pallas_call | solution.py:560
  87.0 0.0 copy-done.2
  87.0 0.0 copy-done.7
  87.0 23.3 %propagate.3 = (f32[2,512,768]{2,1,0:T(8,128)S(1)}, f32[4,2,256,256]{3,2,1,0:T(8,128)S(1)}) custom-call(s32[6,2]{1,0:T(8,128)S(1)} %add_subtract_fusion.offs, bf16[2,512,768]{2,1,0:T(8,128)(2,1)S(1)} %get-tuple-element.14.ext, f32[4,2,256,256]{3,2,1,0:T(8,128)S(1)} %bitcast.7, f32[6,256,256]{2,1,0:T(8,128)S(1)} %copy-done.2, bf16[512,512]{1,0:T(8,128)(2,1)S(1)} %copy-done.7, ...), custom_call_target="tpu_custom_call" | custom-call | tf_op jit(solution)/shard_map/propagate/pallas_call | solution.py:144
  110.3 30.1 %last_exchange.1 = (f32[2,256,512]{2,1,0:T(8,128)S(1)}, bf16[2048,256]{1,0:T(8,128)(2,1)S(1)}) custom-call(f32[2,512,768]{2,1,0:T(8,128)S(1)} %get-tuple-element.16.grad, f32[2048,256]{1,0:T(8,128)S(1)} %bitcast.9, f32[2,256,512]{2,1,0:T(8,128)S(1)} %get-tuple-element.13.tile, f32[2048,256]{1,0:T(8,128)S(1)} %get-tuple-element.15.probe), custom_call_target="tpu_custom_call" | custom-call | tf_op jit(solution)/shard_map/last_exchange/pallas_call | solution.py:560
  140.4 1.2 add.18
  141.6 1.6 %multiply_add_fusion = f32[2048,256]{1,0:T(8,128)} fusion(f32[2048,256]{1,0:T(8,128)S(1)} %get-tuple-element.15.probe, bf16[2048,256]{1,0:T(8,128)(2,1)S(1)} %get-tuple-element.19), kind=kLoop, calls=%fused_computation | loop fusion | flops 1572864 | bytes 5242880 | tf_op jit(solution)/shard_map/add | solution.py:586
  (1 shorter events, 0.0 us)
Async XLA Ops:
  0.6 15.2 %copy-start = (f32[4,2,256,256]{3,2,1,0:T(8,128)S(1)}, f32[4,2,256,256]{3,2,1,0:T(8,128)}, u32[]{:S(2)}) copy-start(f32[4,2,256,256]{3,2,1,0:T(8,128)} %probe_in.1) | copy-start | bytes 6291460
  1.6 1.2 copy-start.3
  2.9 13.0 %copy-start.5 = (bf16[512,512]{1,0:T(8,128)(2,1)S(1)}, bf16[512,512]{1,0:T(8,128)(2,1)}, u32[]{:S(2)}) copy-start(bf16[512,512]{1,0:T(8,128)(2,1)} %constant.33.clone.minus) | copy-start | bytes 1572868
  15.9 1.4 copy-start.1
  17.3 1.0 copy-start.6
  18.3 23.6 %copy-start.4 = (f32[2,256,512]{2,1,0:T(8,128)S(1)}, f32[2,256,512]{2,1,0:T(8,128)}, u32[]{:S(2)}) copy-start(f32[2,256,512]{2,1,0:T(8,128)} %tile.3) | copy-start | bytes 3145732
  42.0 45.0 %copy-start.2 = (f32[6,256,256]{2,1,0:T(8,128)S(1)}, f32[6,256,256]{2,1,0:T(8,128)}, u32[]{:S(2)}) copy-start(f32[6,256,256]{2,1,0:T(8,128)} %amp.3) | copy-start | bytes 4718596
  42.0 45.0 %copy-start.7 = (bf16[512,512]{1,0:T(8,128)(2,1)S(1)}, bf16[512,512]{1,0:T(8,128)(2,1)}, u32[]{:S(2)}) copy-start(bf16[512,512]{1,0:T(8,128)(2,1)} %constant.32.clone.plus) | copy-start | bytes 1572868

commit v2 on v1

--- a/solution.py
+++ b/solution.py
@@ -19,6 +19,7 @@
 TR, TC = 256, 512
 ER, EC = TR + S, TC + S
 MODES, COUNT = 4, 6
+GROUP = 3
 ROWS = MODES * 2 * S
 CHUNKS = 2
 CHUNK = ROWS // CHUNKS
@@ -49,9 +50,11 @@
 
 
 def propagate_body(
-    offs, ext, probe_in, amp, plus, minus, grad, probe_grad, ext32, probe, patch, wave, half, far
+    offs, ext, probe_in, amp, plus, minus, grad, probe_grad,
+    ext32, probe, patches, waves, halves, fars,
 ):
-    n = pl.program_id(0)
+    turn = pl.program_id(0)
+    me = Place()
 
     def by_rows(ref, value):
         @pl.loop(0, ref.shape[0] // 64)
@@ -59,7 +62,7 @@
             rows = pl.ds(i * 64, 64)
             ref[rows] = value(rows)
 
-    @pl.when(n == 0)
+    @pl.when(turn == 0)
     def _():
         for p in range(2):
             by_rows(grad.at[p], lambda rows: jnp.zeros((64, EC), F32))
@@ -70,69 +73,86 @@
                     probe.at[m, p], lambda rows: probe_in[m, p, rows].astype(BF16).astype(F32)
                 )
 
-    row, col = offs[n, 0], offs[n, 1]
-    row_base = pl.multiple_of((row // 8) * 8, 8)
-    row_shift = row - row_base
-    col_block = col // 128
-    shift = col - col_block * 128
-    rows = pl.ds(row_base, S + 8)
-
-    def cols(i):
-        return pl.ds(pl.multiple_of((col_block + i) * 128, 128), 128)
-
     lane = lax.broadcasted_iota(jnp.int32, (S + 8, 128), 1)
-    for p in range(2):
-        x = [pltpu.roll(ext32[p, rows, cols(i)], lax.rem(128 - shift, 128), 1) for i in range(3)]
-        for i in range(2):
-            joined = jnp.where(lane < 128 - shift, x[i], x[i + 1])
-            joined = pltpu.roll(joined, lax.rem(S + 8 - row_shift, S + 8), 0)
-            patch[p, :, i * 128 : (i + 1) * 128] = joined[:S]
-    for m in range(MODES):
-        qr, qi = probe[m, 0], probe[m, 1]
-        pr, pi = patch[0], patch[1]
-        wave[m, :S, :] = (qr * pr - qi * pi).astype(BF16)
-        wave[m, S:, :] = (qr * pi + qi * pr).astype(BF16)
-        mid = jnp.dot(plus[...], wave[m], preferred_element_type=F32).astype(BF16)
+
+    def place(a):
+        row = offs[0, turn * GROUP + a] - me.dp * TR + H
+        col = offs[1, turn * GROUP + a] - me.obj * TC + H
+        row_base = pl.multiple_of((row // 8) * 8, 8)
+        col_block = col // 128
+
+        def cols(i):
+            return pl.ds(pl.multiple_of((col_block + i) * 128, 128), 128)
+
+        return pl.ds(row_base, S + 8), row - row_base, cols, col - col_block * 128
+
+    def left(table, wave, half, m):
+        mid = jnp.dot(table[...], wave[m], preferred_element_type=F32).astype(BF16)
         half[m * S : (m + 1) * S, :S] = mid[:S]
         half[m * S : (m + 1) * S, S:] = mid[S:]
-    far[...] = jnp.dot(half[...], minus[...], preferred_element_type=F32)
-    intensity = None
-    for m in range(MODES):
-        fr, fi = far[m * S : (m + 1) * S, :S], far[m * S : (m + 1) * S, S:]
-        term = fr * fr + fi * fi
-        intensity = term if intensity is None else intensity + term
-    ratio = amp[0] * jnp.minimum(lax.rsqrt(intensity), 1.0) - 1.0
-    for m in range(MODES):
-        wave[m, :S, :] = (far[m * S : (m + 1) * S, :S] * ratio).astype(BF16)
-        wave[m, S:, :] = (far[m * S : (m + 1) * S, S:] * ratio).astype(BF16)
-        mid = jnp.dot(minus[...], wave[m], preferred_element_type=F32).astype(BF16)
-        half[m * S : (m + 1) * S, :S] = mid[:S]
-        half[m * S : (m + 1) * S, S:] = mid[S:]
-    far[...] = jnp.dot(half[...], plus[...], preferred_element_type=F32)
-    gr = gi = None
-    for m in range(MODES):
-        cr, ci = far[m * S : (m + 1) * S, :S], far[m * S : (m + 1) * S, S:]
-        qr, qi = probe[m, 0], probe[m, 1]
-        a, b = qr * cr + qi * ci, qr * ci - qi * cr
-        gr = a if gr is None else gr + a
-        gi = b if gi is None else gi + b
-        pr, pi = patch[0], patch[1]
-        probe_grad[m, 0] += pr * cr + pi * ci
-        probe_grad[m, 1] += pr * ci - pi * cr
-    for p, value in enumerate((gr, gi)):
-        value = jnp.concatenate([value, jnp.zeros((8, S), F32)], 0)
-        x = [
-            pltpu.roll(pltpu.roll(value[:, i * 128 : (i + 1) * 128], row_shift, 0), shift, 1)
-            for i in range(2)
-        ]
-        zero = jnp.zeros_like(x[0])
-        parts = (
-            jnp.where(lane >= shift, x[0], zero),
-            jnp.where(lane >= shift, x[1], x[0]),
-            jnp.where(lane >= shift, zero, x[1]),
-        )
-        for i in range(3):
-            grad[p, rows, cols(i)] += parts[i]
+
+    def forward(a):
+        patch, wave, half, far = patches.at[a], waves.at[a], halves.at[a], fars.at[a]
+        rows, row_shift, cols, shift = place(a)
+        for p in range(2):
+            x = [
+                pltpu.roll(ext32[p, rows, cols(i)], lax.rem(128 - shift, 128), 1) for i in range(3)
+            ]
+            for i in range(2):
+                joined = jnp.where(lane < 128 - shift, x[i], x[i + 1])
+                joined = pltpu.roll(joined, lax.rem(S + 8 - row_shift, S + 8), 0)
+                patch[p, :, i * 128 : (i + 1) * 128] = joined[:S]
+        for m in range(MODES):
+            qr, qi = probe[m, 0], probe[m, 1]
+            pr, pi = patch[0], patch[1]
+            wave[m, :S, :] = (qr * pr - qi * pi).astype(BF16)
+            wave[m, S:, :] = (qr * pi + qi * pr).astype(BF16)
+            left(plus, wave, half, m)
+        far[...] = jnp.dot(half[...], minus[...], preferred_element_type=F32)
+
+    def backward(a):
+        patch, wave, half, far = patches.at[a], waves.at[a], halves.at[a], fars.at[a]
+        rows, row_shift, cols, shift = place(a)
+        intensity = None
+        for m in range(MODES):
+            fr, fi = far[m * S : (m + 1) * S, :S], far[m * S : (m + 1) * S, S:]
+            term = fr * fr + fi * fi
+            intensity = term if intensity is None else intensity + term
+        ratio = amp[a] * jnp.minimum(lax.rsqrt(intensity), 1.0) - 1.0
+        for m in range(MODES):
+            wave[m, :S, :] = (far[m * S : (m + 1) * S, :S] * ratio).astype(BF16)
+            wave[m, S:, :] = (far[m * S : (m + 1) * S, S:] * ratio).astype(BF16)
+            left(minus, wave, half, m)
+        far[...] = jnp.dot(half[...], plus[...], preferred_element_type=F32)
+        gr = gi = None
+        for m in range(MODES):
+            cr, ci = far[m * S : (m + 1) * S, :S], far[m * S : (m + 1) * S, S:]
+            qr, qi = probe[m, 0], probe[m, 1]
+            to_re, to_im = qr * cr + qi * ci, qr * ci - qi * cr
+            gr = to_re if gr is None else gr + to_re
+            gi = to_im if gi is None else gi + to_im
+            pr, pi = patch[0], patch[1]
+            probe_grad[m, 0] += pr * cr + pi * ci
+            probe_grad[m, 1] += pr * ci - pi * cr
+        for p, value in enumerate((gr, gi)):
+            value = jnp.concatenate([value, jnp.zeros((8, S), F32)], 0)
+            x = [
+                pltpu.roll(pltpu.roll(value[:, i * 128 : (i + 1) * 128], row_shift, 0), shift, 1)
+                for i in range(2)
+            ]
+            zero = jnp.zeros_like(x[0])
+            parts = (
+                jnp.where(lane >= shift, x[0], zero),
+                jnp.where(lane >= shift, x[1], x[0]),
+                jnp.where(lane >= shift, zero, x[1]),
+            )
+            for i in range(3):
+                grad[p, rows, cols(i)] += parts[i]
+
+    for a in range(GROUP):
+        forward(a)
+    for a in range(GROUP):
+        backward(a)
 
 
 def propagate(offs, ext, probe, amplitude):
@@ -145,11 +165,11 @@
         propagate_body,
         grid_spec=pltpu.PrefetchScalarGridSpec(
             num_scalar_prefetch=1,
-            grid=(COUNT,),
+            grid=(COUNT // GROUP,),
             in_specs=[
                 whole(2, ER, EC),
                 whole(MODES, 2, S, S),
-                pl.BlockSpec((1, S, S), lambda n, o: (n, 0, 0)),
+                pl.BlockSpec((GROUP, S, S), lambda n, o: (n, 0, 0)),
                 whole(2 * S, 2 * S),
                 whole(2 * S, 2 * S),
             ],
@@ -157,10 +177,10 @@
             scratch_shapes=[
                 pltpu.VMEM((2, ER, EC), F32),
                 pltpu.VMEM((MODES, 2, S, S), F32),
-                pltpu.VMEM((2, S, S), F32),
-                pltpu.VMEM((MODES, 2 * S, S), BF16),
-                pltpu.VMEM((MODES * S, 2 * S), BF16),
-                pltpu.VMEM((MODES * S, 2 * S), F32),
+                pltpu.VMEM((GROUP, 2, S, S), F32),
+                pltpu.VMEM((GROUP, MODES, 2 * S, S), BF16),
+                pltpu.VMEM((GROUP, MODES * S, 2 * S), BF16),
+                pltpu.VMEM((GROUP, MODES * S, 2 * S), F32),
             ],
         ),
         out_shape=[
@@ -168,7 +188,7 @@
             jax.ShapeDtypeStruct((MODES, 2, S, S), F32),
         ],
         compiler_params=pltpu.CompilerParams(
-            dimension_semantics=("arbitrary",), vmem_limit_bytes=32 * MIB
+            dimension_semantics=("arbitrary",), vmem_limit_bytes=36 * MIB
         ),
         name="propagate",
     )(offs, ext, probe, amplitude, jnp.asarray(plus), jnp.asarray(minus))
@@ -289,13 +309,21 @@
             pl.when(self.me.has(a, b))(copy.wait_send)
 
 
-def halo_body(tile, ext, sems):
+def halo_body(tile, ext, local, sems, local_sems):
     me = Place()
+    loads = [
+        pltpu.make_async_copy(tile.at[plane], local.at[plane], local_sems.at[plane])
+        for plane in range(2)
+    ]
+    for load in loads:
+        load.start()
     expected = signal_all(me, False)
     halos = [Halo(me, ext, sems, plane) for plane in range(2)]
     for plane in range(2):
-        ext[plane, H : H + TR, H : H + TC] = tile[plane].astype(BF16)
         halos[plane].clear(ext, plane)
+    for plane in range(2):
+        loads[plane].wait()
+        ext[plane, H : H + TR, H : H + TC] = local[plane].astype(BF16)
     wait_all(expected)
     for halo in halos:
         halo.start()
@@ -307,9 +335,13 @@
     return pl.pallas_call(
         halo_body,
         out_shape=jax.ShapeDtypeStruct((2, ER, EC), BF16),
-        in_specs=[pl.BlockSpec(memory_space=pltpu.VMEM)],
+        in_specs=[pl.BlockSpec(memory_space=pltpu.HBM)],
         out_specs=pl.BlockSpec(memory_space=pltpu.VMEM),
-        scratch_shapes=[pltpu.SemaphoreType.DMA((2, 16))],
+        scratch_shapes=[
+            pltpu.VMEM((2, TR, TC), F32),
+            pltpu.SemaphoreType.DMA((2, 16)),
+            pltpu.SemaphoreType.DMA((2,)),
+        ],
         compiler_params=pltpu.CompilerParams(
             collective_id=0, has_side_effects=True, vmem_limit_bytes=16 * MIB
         ),
@@ -570,20 +602,53 @@
     )(grad, probe_grad.reshape(ROWS, S), tile, probe)
 
 
+def finish_body(tile, step, probe, total, tile_out, probe_out, tile_new, probe_new, sems):
+    copies = []
+    for p in range(2):
+        tile_new[p] = tile[p] + step[p]
+        copies.append(pltpu.make_async_copy(tile_new.at[p], tile_out.at[p], sems.at[p]))
+        copies[-1].start()
+    for i in range(4):
+        part = pl.ds(i * 512, 512)
+        probe_new[part] = probe[part] + total[part].astype(F32) / (COUNT * 128)
+        copies.append(
+            pltpu.make_async_copy(probe_new.at[part], probe_out.at[part], sems.at[2 + i])
+        )
+        copies[-1].start()
+    for copy in copies:
+        copy.wait()
+
+
+def finish(tile, step, probe, total):
+    vmem, hbm = (pl.BlockSpec(memory_space=space) for space in (pltpu.VMEM, pltpu.HBM))
+    return pl.pallas_call(
+        finish_body,
+        out_shape=[
+            jax.ShapeDtypeStruct(tile.shape, F32),
+            jax.ShapeDtypeStruct(probe.shape, F32),
+        ],
+        in_specs=[vmem] * 4,
+        out_specs=[hbm] * 2,
+        scratch_shapes=[
+            pltpu.VMEM(tile.shape, F32),
+            pltpu.VMEM(probe.shape, F32),
+            pltpu.SemaphoreType.DMA((6,)),
+        ],
+        compiler_params=pltpu.CompilerParams(vmem_limit_bytes=16 * MIB),
+        name="finish",
+    )(tile, step, probe, total)
+
+
 def shards(object_field, probe_modes, amplitude, offsets):
-    dp = lax.axis_index(AXES[:2])
-    obj = lax.axis_index(AXES[2:])
-    offs = offsets + H - jnp.stack([dp * TR, obj * TC]).astype(jnp.int32)
     probe = probe_modes.reshape(ROWS, S)
     tile = object_field
     ext = first_halo(tile)
     for turn in range(ITERS):
-        grad, probe_grad = propagate(offs, ext, probe.reshape(MODES, 2, S, S), amplitude)
+        grad, probe_grad = propagate(offsets.T, ext, probe.reshape(MODES, 2, S, S), amplitude)
         last = turn + 1 == ITERS
         results = exchange(last, grad, probe_grad, tile, probe)
         if last:
-            tile = tile + results[0]
-            probe = probe + results[1].astype(F32) / (COUNT * 128)
+            tile, probe = finish(tile, results[0], probe, results[1])
         else:
             tile, probe, ext = results
     return tile, probe.reshape(MODES, 2, S, S)

time: 143 us -> 136 us (0.951)
  Pallas kernels: 135 us -> 131 us
  other arithmetic: 2.82 us -> 0 us
    pallas_call x2, Pallas kernels: 46.9 us -> 40.8 us  [propagate(): pl.pallas_call(propagate_body, grid_spec=pltpu.PrefetchScalarGridSpec(num...]
    add x2 -> x0, other arithmetic: 2.74 us -> none  [the longest x1 1.56 us: shards(): probe = probe + results[1].astype(F32) / (COUNT * 128)]
    pallas_call x0 -> x1, Pallas kernels: none -> 1.76 us  [finish(): pl.pallas_call(finish_body, out_shape=[jax.ShapeDtypeStruct(tile.shape, F...]
    unnamed x17 -> x18, local copies, waits for them, and re-layouts: 4.59 us -> 3.84 us
where the time goes in v2:
time: 136 us
  Pallas kernels  131 us (96%)
  local copies, waits for them, and re-layouts  3.84 us (3%)
    pallas_call x2, Pallas kernels, exchange(): pl.pallas_call(functools.partial(exchange_body, last), out_shape=[jax.Sha...  75.3 us
    pallas_call x2, Pallas kernels, propagate(): pl.pallas_call(propagate_body, grid_spec=pltpu.PrefetchScalarGridSpec(num...  40.8 us
    pallas_call x1, Pallas kernels, first_halo(): pl.pallas_call(halo_body, out_shape=jax.ShapeDtypeStruct((2, ER, EC), BF1...  13.1 us
    unnamed x18, local copies, waits for them, and re-layouts  3.84 us

profile of v2, /device:TPU:1, one launch (start us, length us, event | category | flops | bytes accessed | tf_op | source)
XLA Modules:
  0.0 135.7 jit_solution(13373389057915767809)
XLA Ops:
  0.6 0.0 copy-start
  0.6 0.0 copy-start.3
  0.7 1.4 %copy-done.3 = f32[2,256,512]{2,1,0:T(8,128)S(1)} copy-done((f32[2,256,512]{2,1,0:T(8,128)S(1)}, f32[2,256,512]{2,1,0:T(8,128)}, u32[]{:S(2)}) %copy-start.3) | copy-done | bytes 1048600
  2.0 0.0 copy-start.5
  2.0 0.0 copy-start.8
  2.0 13.1 %first_halo.1.ext = bf16[2,512,768]{2,1,0:T(8,128)(2,1)S(1)} custom-call(f32[2,256,512]{2,1,0:T(8,128)S(1)} %copy-done.3), custom_call_target="tpu_custom_call" | custom-call | tf_op jit(solution)/shard_map/first_halo/pallas_call | solution.py:335
  15.1 0.0 copy-done
  15.2 0.0 copy-done.5
  15.2 0.0 copy-done.8
  15.2 0.0 copy-start.1
  15.2 1.4 %copy-done.1 = f32[6,256,256]{2,1,0:T(8,128)S(1)} copy-done((f32[6,256,256]{2,1,0:T(8,128)S(1)}, f32[6,256,256]{2,1,0:T(8,128)}, u32[]{:S(2)}) %copy-start.1) | copy-done | bytes 1572888
  16.6 0.0 copy-start.6
  16.6 1.0 copy-done.6
  17.6 0.0 copy-start.4
  17.6 20.3 %propagate.2 = (f32[2,512,768]{2,1,0:T(8,128)S(1)}, f32[4,2,256,256]{3,2,1,0:T(8,128)S(1)}) custom-call(s32[2,6]{1,0:T(2,128)S(1)} %bitcast.10, bf16[2,512,768]{2,1,0:T(8,128)(2,1)S(1)} %first_halo.1.ext, f32[4,2,256,256]{3,2,1,0:T(8,128)S(1)} %copy-done, f32[6,256,256]{2,1,0:T(8,128)S(1)} %copy-done.1, bf16[512,512]{1,0:T(8,128)(2,1)S(1)} %copy-done.6, ...), custom_call_target="tpu_custom_call" | custom-call | tf_op jit(solution)/shard_map/propagate/pallas_call | solution.py:164
  37.9 0.0 copy-done.4
  38.0 0.0 copy-start.2
  38.0 0.0 copy-start.7
  38.0 45.7 %exchange.1 = (f32[2,256,512]{2,1,0:T(8,128)S(1)}, f32[2048,256]{1,0:T(8,128)S(1)}, bf16[2,512,768]{2,1,0:T(8,128)(2,1)S(1)}) custom-call(f32[2,512,768]{2,1,0:T(8,128)S(1)} %get-tuple-element.13.grad, f32[2048,256]{1,0:T(8,128)S(1)} %bitcast.9, f32[2,256,512]{2,1,0:T(8,128)S(1)} %copy-done.4, f32[2048,256]{1,0:T(8,128)S(1)} %bitcast.7), custom_call_target="tpu_custom_call" | custom-call | tf_op jit(solution)/shard_map/exchange/pallas_call | solution.py:592
  83.6 0.0 copy-done.2
  83.7 0.0 copy-done.7
  83.7 20.4 %propagate.3 = (f32[2,512,768]{2,1,0:T(8,128)S(1)}, f32[4,2,256,256]{3,2,1,0:T(8,128)S(1)}) custom-call(s32[2,6]{1,0:T(2,128)S(1)} %bitcast.11, bf16[2,512,768]{2,1,0:T(8,128)(2,1)S(1)} %get-tuple-element.16.ext, f32[4,2,256,256]{3,2,1,0:T(8,128)S(1)} %bitcast.6, f32[6,256,256]{2,1,0:T(8,128)S(1)} %copy-done.2, bf16[512,512]{1,0:T(8,128)(2,1)S(1)} %copy-done.7, ...), custom_call_target="tpu_custom_call" | custom-call | tf_op jit(solution)/shard_map/propagate/pallas_call | solution.py:164
  104.1 29.6 %last_exchange.1 = (f32[2,256,512]{2,1,0:T(8,128)S(1)}, bf16[2048,256]{1,0:T(8,128)(2,1)S(1)}) custom-call(f32[2,512,768]{2,1,0:T(8,128)S(1)} %get-tuple-element.18.grad, f32[2048,256]{1,0:T(8,128)S(1)} %bitcast.8, f32[2,256,512]{2,1,0:T(8,128)S(1)} %get-tuple-element.15.tile, f32[2048,256]{1,0:T(8,128)S(1)} %get-tuple-element.17.probe), custom_call_target="tpu_custom_call" | custom-call | tf_op jit(solution)/shard_map/last_exchange/pallas_call | solution.py:592
  133.8 1.8 %finish.1 = (f32[2,256,512]{2,1,0:T(8,128)}, f32[2048,256]{1,0:T(8,128)}) custom-call(f32[2,256,512]{2,1,0:T(8,128)S(1)} %get-tuple-element.15.tile, f32[2,256,512]{2,1,0:T(8,128)S(1)} %get-tuple-element.20.step, f32[2048,256]{1,0:T(8,128)S(1)} %get-tuple-element.17.probe, bf16[2048,256]{1,0:T(8,128)(2,1)S(1)} %get-tuple-element.21.total), custom_call_target="tpu_custom_call" | custom-call | tf_op jit(solution)/shard_map/finish/pallas_call | solution.py:624
Async XLA Ops:
  0.6 14.5 %copy-start = (f32[4,2,256,256]{3,2,1,0:T(8,128)S(1)}, f32[4,2,256,256]{3,2,1,0:T(8,128)}, u32[]{:S(2)}) copy-start(f32[4,2,256,256]{3,2,1,0:T(8,128)} %probe_in.1) | copy-start | bytes 6291460
  0.6 1.4 %copy-start.3 = (f32[2,256,512]{2,1,0:T(8,128)S(1)}, f32[2,256,512]{2,1,0:T(8,128)}, u32[]{:S(2)}) copy-start(f32[2,256,512]{2,1,0:T(8,128)} %tile.3) | copy-start | bytes 3145732
  2.0 13.1 %copy-start.5 = (bf16[512,512]{1,0:T(8,128)(2,1)S(1)}, bf16[512,512]{1,0:T(8,128)(2,1)}, u32[]{:S(2)}) copy-start(bf16[512,512]{1,0:T(8,128)(2,1)} %constant.5.clone.minus) | copy-start | bytes 1572868
  2.0 13.1 %copy-start.8 = (s32[6,2]{0,1:T(2,128)S(1)}, s32[6,2]{0,1:T(2,128)}, u32[]{:S(2)}) copy-start(s32[6,2]{0,1:T(2,128)} %param.11) | copy-start | bytes 148
  15.2 1.4 %copy-start.1 = (f32[6,256,256]{2,1,0:T(8,128)S(1)}, f32[6,256,256]{2,1,0:T(8,128)}, u32[]{:S(2)}) copy-start(f32[6,256,256]{2,1,0:T(8,128)} %amp.3) | copy-start | bytes 4718596
  16.6 1.0 copy-start.6
  17.6 20.3 %copy-start.4 = (f32[2,256,512]{2,1,0:T(8,128)S(1)}, f32[2,256,512]{2,1,0:T(8,128)}, u32[]{:S(2)}) copy-start(f32[2,256,512]{2,1,0:T(8,128)} %tile.3) | copy-start | bytes 3145732
  38.0 45.7 %copy-start.2 = (f32[6,256,256]{2,1,0:T(8,128)S(1)}, f32[6,256,256]{2,1,0:T(8,128)}, u32[]{:S(2)}) copy-start(f32[6,256,256]{2,1,0:T(8,128)} %amp.3) | copy-start | bytes 4718596
  38.0 45.7 %copy-start.7 = (bf16[512,512]{1,0:T(8,128)(2,1)S(1)}, bf16[512,512]{1,0:T(8,128)(2,1)}, u32[]{:S(2)}) copy-start(bf16[512,512]{1,0:T(8,128)(2,1)} %constant.4.clone.plus) | copy-start | bytes 1572868

commit v3 on v2

--- a/solution.py
+++ b/solution.py
@@ -46,12 +46,12 @@
     angle = 2.0 * np.pi * (counter[:, None] * counter[None, :] % S) / S
     re = (np.cos(angle) / 16.0).astype(np.float32).astype(ml_dtypes.bfloat16)
     im = (-np.sin(angle) / 16.0).astype(np.float32).astype(ml_dtypes.bfloat16)
-    return np.block([[re, -im], [im, re]]), np.block([[re, im], [-im, re]])
+    return np.block([[re, -im], [im, re]])
 
 
 def propagate_body(
-    offs, ext, probe_in, amp, plus, minus, grad, probe_grad,
-    ext32, probe, patches, waves, halves, fars,
+    offs, ext, probe_in, amp, plus, grad, probe_grad,
+    ext32, probe, patches, waves, halves, fars, minus,
 ):
     turn = pl.program_id(0)
     me = Place()
@@ -64,6 +64,10 @@
 
     @pl.when(turn == 0)
     def _():
+        minus[:S, :S] = plus[:S, :S]
+        minus[S:, S:] = plus[S:, S:]
+        minus[:S, S:] = plus[S:, :S]
+        minus[S:, :S] = plus[:S, S:]
         for p in range(2):
             by_rows(grad.at[p], lambda rows: jnp.zeros((64, EC), F32))
             by_rows(ext32.at[p], lambda rows: ext[p, rows].astype(F32))
@@ -156,7 +160,6 @@
 
 
 def propagate(offs, ext, probe, amplitude):
-    plus, minus = dft_tables()
 
     def whole(*shape):
         return pl.BlockSpec(shape, lambda n, o: (0,) * len(shape))
@@ -171,7 +174,6 @@
                 whole(MODES, 2, S, S),
                 pl.BlockSpec((GROUP, S, S), lambda n, o: (n, 0, 0)),
                 whole(2 * S, 2 * S),
-                whole(2 * S, 2 * S),
             ],
             out_specs=[whole(2, ER, EC), whole(MODES, 2, S, S)],
             scratch_shapes=[
@@ -181,6 +183,7 @@
                 pltpu.VMEM((GROUP, MODES, 2 * S, S), BF16),
                 pltpu.VMEM((GROUP, MODES * S, 2 * S), BF16),
                 pltpu.VMEM((GROUP, MODES * S, 2 * S), F32),
+                pltpu.VMEM((2 * S, 2 * S), BF16),
             ],
         ),
         out_shape=[
@@ -191,7 +194,7 @@
             dimension_semantics=("arbitrary",), vmem_limit_bytes=36 * MIB
         ),
         name="propagate",
-    )(offs, ext, probe, amplitude, jnp.asarray(plus), jnp.asarray(minus))
+    )(offs, ext, probe, amplitude, jnp.asarray(dft_tables()))
 
 
 NEAR = [(a, b) for a in (-1, 0, 1) for b in (-1, 0, 1) if (a, b) != (0, 0)]
@@ -342,6 +345,7 @@
             pltpu.SemaphoreType.DMA((2, 16)),
             pltpu.SemaphoreType.DMA((2,)),
         ],
+        cost_estimate=pl.CostEstimate(flops=10**10, bytes_accessed=10**6, transcendentals=0),
         compiler_params=pltpu.CompilerParams(
             collective_id=0, has_side_effects=True, vmem_limit_bytes=16 * MIB
         ),

time: 136 us -> 133 us (0.978)
  local copies, waits for them, and re-layouts: 3.84 us -> 1.23 us
    unnamed x18 -> x10, local copies, waits for them, and re-layouts: 3.84 us -> 1.23 us
where the time goes in v3:
time: 133 us; the launch traced here: 132 us
  Pallas kernels  130 us (98%)
    pallas_call x2, Pallas kernels, exchange(): pl.pallas_call(functools.partial(exchange_body, last), out_shape=[jax.Sha...  74.9 us
    pallas_call x2, Pallas kernels, propagate(): pl.pallas_call(propagate_body, grid_spec=pltpu.PrefetchScalarGridSpec(num...  40.4 us
    pallas_call x1, Pallas kernels, first_halo(): pl.pallas_call(halo_body, out_shape=jax.ShapeDtypeStruct((2, ER, EC), BF1...  13.2 us

profile of v3, /device:TPU:1, one launch (start us, length us, event | category | flops | bytes accessed | tf_op | source)
XLA Modules:
  0.0 132.3 jit_solution(9118227525086598908)
XLA Ops:
  0.6 0.0 copy-start.3
  0.6 1.2 copy-done.3
  1.9 0.0 copy-start
  1.9 0.0 copy-start.1
  1.9 0.0 copy-start.2
  1.9 0.0 copy-start.4
  1.9 13.2 %first_halo.1.ext = bf16[2,512,768]{2,1,0:T(8,128)(2,1)S(1)} custom-call(f32[2,256,512]{2,1,0:T(8,128)S(1)} %copy-done.3), custom_call_target="tpu_custom_call" | custom-call | flops 10000000000 | bytes 1000000 | tf_op jit(solution)/shard_map/first_halo/pallas_call | solution.py:338
  15.1 0.0 copy-done
  15.1 0.0 copy-done.1
  15.1 0.0 copy-done.2
  15.1 0.0 copy-done.4
  15.1 20.3 %propagate.2 = (f32[2,512,768]{2,1,0:T(8,128)S(1)}, f32[4,2,256,256]{3,2,1,0:T(8,128)S(1)}) custom-call(s32[2,6]{1,0:T(2,128)S(1)} %bitcast.10, bf16[2,512,768]{2,1,0:T(8,128)(2,1)S(1)} %first_halo.1.ext, f32[4,2,256,256]{3,2,1,0:T(8,128)S(1)} %copy-done, f32[6,256,256]{2,1,0:T(8,128)S(1)} %copy-done.1, bf16[512,512]{1,0:T(8,128)(2,1)S(1)} %copy-done.2), custom_call_target="tpu_custom_call" | custom-call | tf_op jit(solution)/shard_map/propagate/pallas_call | solution.py:167
  35.4 45.1 %exchange.1 = (f32[2,256,512]{2,1,0:T(8,128)S(1)}, f32[2048,256]{1,0:T(8,128)S(1)}, bf16[2,512,768]{2,1,0:T(8,128)(2,1)S(1)}) custom-call(f32[2,512,768]{2,1,0:T(8,128)S(1)} %get-tuple-element.13.grad, f32[2048,256]{1,0:T(8,128)S(1)} %bitcast.8, f32[2,256,512]{2,1,0:T(8,128)S(1)} %copy-done.3, f32[2048,256]{1,0:T(8,128)S(1)} %bitcast.7), custom_call_target="tpu_custom_call" | custom-call | tf_op jit(solution)/shard_map/exchange/pallas_call | solution.py:596
  80.5 20.1 %propagate.3 = (f32[2,512,768]{2,1,0:T(8,128)S(1)}, f32[4,2,256,256]{3,2,1,0:T(8,128)S(1)}) custom-call(s32[2,6]{1,0:T(2,128)S(1)} %bitcast.11, bf16[2,512,768]{2,1,0:T(8,128)(2,1)S(1)} %get-tuple-element.16.ext, f32[4,2,256,256]{3,2,1,0:T(8,128)S(1)} %bitcast.6, f32[6,256,256]{2,1,0:T(8,128)S(1)} %copy-done.1, bf16[512,512]{1,0:T(8,128)(2,1)S(1)} %copy-done.2), custom_call_target="tpu_custom_call" | custom-call | tf_op jit(solution)/shard_map/propagate/pallas_call | solution.py:167
  100.6 29.8 %last_exchange.1 = (f32[2,256,512]{2,1,0:T(8,128)S(1)}, bf16[2048,256]{1,0:T(8,128)(2,1)S(1)}) custom-call(f32[2,512,768]{2,1,0:T(8,128)S(1)} %get-tuple-element.18.grad, f32[2048,256]{1,0:T(8,128)S(1)} %bitcast.9, f32[2,256,512]{2,1,0:T(8,128)S(1)} %get-tuple-element.15.tile, f32[2048,256]{1,0:T(8,128)S(1)} %get-tuple-element.17.probe), custom_call_target="tpu_custom_call" | custom-call | tf_op jit(solution)/shard_map/last_exchange/pallas_call | solution.py:596
  130.4 1.8 %finish.1 = (f32[2,256,512]{2,1,0:T(8,128)}, f32[2048,256]{1,0:T(8,128)}) custom-call(f32[2,256,512]{2,1,0:T(8,128)S(1)} %get-tuple-element.15.tile, f32[2,256,512]{2,1,0:T(8,128)S(1)} %get-tuple-element.20.step, f32[2048,256]{1,0:T(8,128)S(1)} %get-tuple-element.17.probe, bf16[2048,256]{1,0:T(8,128)(2,1)S(1)} %get-tuple-element.21.total), custom_call_target="tpu_custom_call" | custom-call | tf_op jit(solution)/shard_map/finish/pallas_call | solution.py:628
Async XLA Ops:
  0.6 1.2 copy-start.3
  1.9 13.2 %copy-start = (f32[4,2,256,256]{3,2,1,0:T(8,128)S(1)}, f32[4,2,256,256]{3,2,1,0:T(8,128)}, u32[]{:S(2)}) copy-start(f32[4,2,256,256]{3,2,1,0:T(8,128)} %probe_in.1) | copy-start | bytes 6291460
  1.9 13.2 %copy-start.1 = (f32[6,256,256]{2,1,0:T(8,128)S(1)}, f32[6,256,256]{2,1,0:T(8,128)}, u32[]{:S(2)}) copy-start(f32[6,256,256]{2,1,0:T(8,128)} %amp.3) | copy-start | bytes 4718596
  1.9 13.2 %copy-start.2 = (bf16[512,512]{1,0:T(8,128)(2,1)S(1)}, bf16[512,512]{1,0:T(8,128)(2,1)}, u32[]{:S(2)}) copy-start(bf16[512,512]{1,0:T(8,128)(2,1)} %constant.2.clone.plus) | copy-start | bytes 1572868
  1.9 13.2 %copy-start.4 = (s32[6,2]{0,1:T(2,128)S(1)}, s32[6,2]{0,1:T(2,128)}, u32[]{:S(2)}) copy-start(s32[6,2]{0,1:T(2,128)} %param.9) | copy-start | bytes 148

commit v4 on v3

--- a/solution.py
+++ b/solution.py
@@ -197,7 +197,7 @@
     )(offs, ext, probe, amplitude, jnp.asarray(dft_tables()))
 
 
-NEAR = [(a, b) for a in (-1, 0, 1) for b in (-1, 0, 1) if (a, b) != (0, 0)]
+NEAR = [(-1, 0), (1, 0), (-1, -1), (-1, 1), (1, -1), (1, 1), (0, -1), (0, 1)]
 
 
 class Place:
@@ -312,21 +312,14 @@
             pl.when(self.me.has(a, b))(copy.wait_send)
 
 
-def halo_body(tile, ext, local, sems, local_sems):
+def halo_body(tile, ext, sems):
     me = Place()
-    loads = [
-        pltpu.make_async_copy(tile.at[plane], local.at[plane], local_sems.at[plane])
-        for plane in range(2)
-    ]
-    for load in loads:
-        load.start()
     expected = signal_all(me, False)
     halos = [Halo(me, ext, sems, plane) for plane in range(2)]
     for plane in range(2):
         halos[plane].clear(ext, plane)
     for plane in range(2):
-        loads[plane].wait()
-        ext[plane, H : H + TR, H : H + TC] = local[plane].astype(BF16)
+        ext[plane, H : H + TR, H : H + TC] = tile[plane].astype(BF16)
     wait_all(expected)
     for halo in halos:
         halo.start()
@@ -338,13 +331,9 @@
     return pl.pallas_call(
         halo_body,
         out_shape=jax.ShapeDtypeStruct((2, ER, EC), BF16),
-        in_specs=[pl.BlockSpec(memory_space=pltpu.HBM)],
+        in_specs=[pl.BlockSpec(memory_space=pltpu.VMEM)],
         out_specs=pl.BlockSpec(memory_space=pltpu.VMEM),
-        scratch_shapes=[
-            pltpu.VMEM((2, TR, TC), F32),
-            pltpu.SemaphoreType.DMA((2, 16)),
-            pltpu.SemaphoreType.DMA((2,)),
-        ],
+        scratch_shapes=[pltpu.SemaphoreType.DMA((2, 16))],
         cost_estimate=pl.CostEstimate(flops=10**10, bytes_accessed=10**6, transcendentals=0),
         compiler_params=pltpu.CompilerParams(
             collective_id=0, has_side_effects=True, vmem_limit_bytes=16 * MIB

time: 133 us -> 132 us (level)
  no operation moved by 1% of the time
where the time goes in v4:
time: 132 us
  Pallas kernels  130 us (98%)
    pallas_call x2, Pallas kernels, exchange(): pl.pallas_call(functools.partial(exchange_body, last), out_shape=[jax.Sha...  73.9 us
    pallas_call x2, Pallas kernels, propagate(): pl.pallas_call(propagate_body, grid_spec=pltpu.PrefetchScalarGridSpec(num...  40.4 us
    pallas_call x1, Pallas kernels, first_halo(): pl.pallas_call(halo_body, out_shape=jax.ShapeDtypeStruct((2, ER, EC), BF1...  14.1 us

profile of v4, /device:TPU:1, one launch (start us, length us, event | category | flops | bytes accessed | tf_op | source)
XLA Modules:
  0.0 132.2 jit_solution(4626900238626738202)
XLA Ops:
  0.6 0.0 copy-start.3
  0.6 1.2 copy-done.3
  1.9 0.0 copy-start
  1.9 0.0 copy-start.1
  1.9 0.0 copy-start.2
  1.9 0.0 copy-start.4
  1.9 14.1 %first_halo.1.ext = bf16[2,512,768]{2,1,0:T(8,128)(2,1)S(1)} custom-call(f32[2,256,512]{2,1,0:T(8,128)S(1)} %copy-done.3), custom_call_target="tpu_custom_call" | custom-call | flops 10000000000 | bytes 1000000 | tf_op jit(solution)/shard_map/first_halo/pallas_call | solution.py:331
  15.9 0.0 copy-done
  16.0 0.0 copy-done.1
  16.0 0.0 copy-done.2
  16.0 0.0 copy-done.4
  16.0 20.3 %propagate.2 = (f32[2,512,768]{2,1,0:T(8,128)S(1)}, f32[4,2,256,256]{3,2,1,0:T(8,128)S(1)}) custom-call(s32[2,6]{1,0:T(2,128)S(1)} %bitcast.10, bf16[2,512,768]{2,1,0:T(8,128)(2,1)S(1)} %first_halo.1.ext, f32[4,2,256,256]{3,2,1,0:T(8,128)S(1)} %copy-done, f32[6,256,256]{2,1,0:T(8,128)S(1)} %copy-done.1, bf16[512,512]{1,0:T(8,128)(2,1)S(1)} %copy-done.2), custom_call_target="tpu_custom_call" | custom-call | tf_op jit(solution)/shard_map/propagate/pallas_call | solution.py:167
  36.3 44.3 %exchange.1 = (f32[2,256,512]{2,1,0:T(8,128)S(1)}, f32[2048,256]{1,0:T(8,128)S(1)}, bf16[2,512,768]{2,1,0:T(8,128)(2,1)S(1)}) custom-call(f32[2,512,768]{2,1,0:T(8,128)S(1)} %get-tuple-element.13.grad, f32[2048,256]{1,0:T(8,128)S(1)} %bitcast.8, f32[2,256,512]{2,1,0:T(8,128)S(1)} %copy-done.3, f32[2048,256]{1,0:T(8,128)S(1)} %bitcast.7), custom_call_target="tpu_custom_call" | custom-call | tf_op jit(solution)/shard_map/exchange/pallas_call | solution.py:585
  80.6 20.1 %propagate.3 = (f32[2,512,768]{2,1,0:T(8,128)S(1)}, f32[4,2,256,256]{3,2,1,0:T(8,128)S(1)}) custom-call(s32[2,6]{1,0:T(2,128)S(1)} %bitcast.11, bf16[2,512,768]{2,1,0:T(8,128)(2,1)S(1)} %get-tuple-element.16.ext, f32[4,2,256,256]{3,2,1,0:T(8,128)S(1)} %bitcast.6, f32[6,256,256]{2,1,0:T(8,128)S(1)} %copy-done.1, bf16[512,512]{1,0:T(8,128)(2,1)S(1)} %copy-done.2), custom_call_target="tpu_custom_call" | custom-call | tf_op jit(solution)/shard_map/propagate/pallas_call | solution.py:167
  100.7 29.6 %last_exchange.1 = (f32[2,256,512]{2,1,0:T(8,128)S(1)}, bf16[2048,256]{1,0:T(8,128)(2,1)S(1)}) custom-call(f32[2,512,768]{2,1,0:T(8,128)S(1)} %get-tuple-element.18.grad, f32[2048,256]{1,0:T(8,128)S(1)} %bitcast.9, f32[2,256,512]{2,1,0:T(8,128)S(1)} %get-tuple-element.15.tile, f32[2048,256]{1,0:T(8,128)S(1)} %get-tuple-element.17.probe), custom_call_target="tpu_custom_call" | custom-call | tf_op jit(solution)/shard_map/last_exchange/pallas_call | solution.py:585
  130.3 1.8 %finish.1 = (f32[2,256,512]{2,1,0:T(8,128)}, f32[2048,256]{1,0:T(8,128)}) custom-call(f32[2,256,512]{2,1,0:T(8,128)S(1)} %get-tuple-element.15.tile, f32[2,256,512]{2,1,0:T(8,128)S(1)} %get-tuple-element.20.step, f32[2048,256]{1,0:T(8,128)S(1)} %get-tuple-element.17.probe, bf16[2048,256]{1,0:T(8,128)(2,1)S(1)} %get-tuple-element.21.total), custom_call_target="tpu_custom_call" | custom-call | tf_op jit(solution)/shard_map/finish/pallas_call | solution.py:617
Async XLA Ops:
  0.6 1.2 copy-start.3
  1.9 14.1 %copy-start = (f32[4,2,256,256]{3,2,1,0:T(8,128)S(1)}, f32[4,2,256,256]{3,2,1,0:T(8,128)}, u32[]{:S(2)}) copy-start(f32[4,2,256,256]{3,2,1,0:T(8,128)} %probe_in.1) | copy-start | bytes 6291460
  1.9 14.1 %copy-start.1 = (f32[6,256,256]{2,1,0:T(8,128)S(1)}, f32[6,256,256]{2,1,0:T(8,128)}, u32[]{:S(2)}) copy-start(f32[6,256,256]{2,1,0:T(8,128)} %amp.3) | copy-start | bytes 4718596
  1.9 14.1 %copy-start.2 = (bf16[512,512]{1,0:T(8,128)(2,1)S(1)}, bf16[512,512]{1,0:T(8,128)(2,1)}, u32[]{:S(2)}) copy-start(bf16[512,512]{1,0:T(8,128)(2,1)} %constant.2.clone.plus) | copy-start | bytes 1572868
  1.9 14.1 %copy-start.4 = (s32[6,2]{0,1:T(2,128)S(1)}, s32[6,2]{0,1:T(2,128)}, u32[]{:S(2)}) copy-start(s32[6,2]{0,1:T(2,128)} %param.9) | copy-start | bytes 148
